TPU v7x, 128 devices: a whole 4x4x4 slice. The times are simulated.
128 devices in a mesh: tm: 4 (over y_hi, core), inputs: 32 (over z, y_lo, x).
Axes of the slice: x: 4, y: 4 (y_hi: 2, y_lo: 2; y = y_hi * 2 + y_lo), z: 4, core: 2. Of those that a mesh axis runs over, the one named last changes fastest.
Arguments:
- voltages: bfloat16 [512, 524288], P('inputs', 'tm'), may hold values from -6 to 6
- filter_taps: float32 [4, 512], replicated, may hold values from -3 to 3
Outputs:
- visibility: float32 [4, 256, 2, 512, 512], P(None, ('tm', 'inputs'))
All inputs are finite; a program needn't handle non-finite values.
Results may differ from a plain program's by a relative error of at most 0.0059.
Values may be sent and summed in bfloat16 or wider, within the bound.
No kernel may reach another device: no remote copies, remote signals or barrier semaphores. Data moves between devices by JAX's collectives and lax.ppermute only.
A program may use at most 128 MiB of HBM per device.

v0:
```python
import math

import jax
import jax.numpy as jnp
from jax import lax
from jax.sharding import PartitionSpec as P

NFFT = 512
TAPS = 4


def shifted(array, axis, by):
    count = lax.axis_size(axis)
    pairs = [(i, i + by) for i in range(count) if 0 <= i + by < count]
    return lax.ppermute(array, axis, pairs)


def fourier_table():
    rows = lax.broadcasted_iota(jnp.int32, (NFFT, NFFT // 2), 0)
    cols = lax.broadcasted_iota(jnp.int32, (NFFT, NFFT // 2), 1)
    phase = (rows * cols % NFFT).astype(jnp.float32) * (2.0 * math.pi / NFFT)
    factor = 1.0 / math.sqrt(NFFT)
    return jnp.stack([jnp.cos(phase) * factor, -jnp.sin(phase) * factor], axis=1).astype(
        jnp.bfloat16
    )


def on_device(voltages, filter_taps):
    local_inputs = voltages.shape[0]
    blocks = voltages.reshape(local_inputs, -1, NFFT)
    spec_count = blocks.shape[1]
    history = shifted(blocks[:, spec_count - (TAPS - 1) :, :], "tm", 1)
    extended = jnp.concatenate([history, blocks], axis=1)
    running = jnp.zeros((local_inputs, spec_count, NFFT), jnp.float32)
    for tap_index in range(TAPS):
        running = running + filter_taps[tap_index][None, None, :] * extended[
            :, tap_index : tap_index + spec_count, :
        ].astype(jnp.float32)
    filtered = running.astype(jnp.bfloat16)
    spectra = jnp.einsum(
        "asn,nrk->kars", filtered, fourier_table(), preferred_element_type=jnp.float32
    ).astype(jnp.bfloat16)
    spectra = spectra.reshape(NFFT // 2, 1, local_inputs, 2 * spec_count)
    moved = lax.all_to_all(spectra, ("tm", "inputs"), split_axis=0, concat_axis=2, tiled=True)
    dump_count = moved.shape[2] // (local_inputs * lax.axis_size("inputs"))
    received = moved.reshape(
        moved.shape[0], dump_count, moved.shape[2] // dump_count, 2 * spec_count
    )
    real_part = received[..., :spec_count]
    imag_part = received[..., spec_count:]
    swapped = jnp.concatenate([imag_part, -real_part], axis=-1)
    stacked = jnp.stack([received, swapped], axis=2)
    visibility = (
        jnp.einsum("cdpar,cdbr->dcpab", stacked, received, preferred_element_type=jnp.float32)
        / spec_count
    )
    return visibility


def solution(mesh):
    in_specs = (P("inputs", "tm"), P())
    out_specs = P(None, ("tm", "inputs"), None, None, None)
    return jax.shard_map(
        on_device, mesh=mesh, in_specs=in_specs, out_specs=out_specs, check_vma=False
    )
```

profile of v0, /device:TPU:1, one launch (start us, length us, event | category | flops | bytes accessed | tf_op | source)
XLA Modules:
  0.0 100.3 jit_solution(10611750987213095952)
XLA Ops:
  0.0 0.0 copy-start
  0.0 3.6 %copy.32 = bf16[2,8,256,512]{3,2,1,0:T(8,128)(2,1)S(1)} copy(bf16[2,8,256,512]{3,1,2,0:T(8,128)(2,1)} %bitcast.35) | data formatting | bytes 8388608
  3.7 6.2 %collective-permute-start = (bf16[16,3,512]{2,1,0:T(4,128)(2,1)S(1)}, bf16[16,3,512]{2,1,0:T(4,128)(2,1)S(1)}, u32[]{:S(2)}, u32[]{:S(2)}) collective-permute-start(bf16[16,3,512]{2,1,0:T(4,128)(2,1)S(1)} %slice.40), channel_id=1, source_target_pairs={{0,32},{32,64},{64,96},{1,33},{33,65},{65,97},{2,34},{34,66},{66,9... | collective-permute-start | bytes 147464 | tf_op jit(solution)/shard_map/ppermute | solution.py:15
  9.9 0.0 copy-done
  9.9 2.2 %multiply_convert_fusion = (bf16[512,1,256]{2,0,1:T(8,128)(2,1)S(1)}, bf16[512,1,256]{2,0,1:T(8,128)(2,1)S(1)}) fusion(), kind=kLoop, calls=%fused_computation.25 | loop fusion | flops 2490368 | bytes 524288 | tf_op jit(solution)/shard_map/convert.1
  12.1 0.0 collective-permute-done
  12.2 4.9 %convert_bitcast_fusion = bf16[256,16,2,256]{0,3,1,2:T(8,128)(2,1)S(1)} fusion(bf16[16,256,512]{2,1,0:T(8,128)(2,1)S(1)} %bitcast.34, f32[512]{0:T(512)S(1)} %bitcast.38, bf16[16,3,512]{2,1,0:T(4,128)(2,1)S(1)} %collective-permute-done, f32[512]{0:T(512)S(1)} %bitcast.39, f32[512]{0:T(512)S(1)} %bitcast.37, f32[512]{0:T(512)S(1)} %bitcast.36, ...), kind=kOutput, calls=%fused_computation.14 | convolution fusion | flops 2194669568 | bytes 8970240 | tf_op jit(solution)/shard_map/asn,nrk->kars/dot_general | solution.py:40
  17.1 2.3 %copy.18 = bf16[256,16,2,256]{0,3,2,1:T(8,128)(2,1)} copy(bf16[256,16,2,256]{0,3,1,2:T(8,128)(2,1)S(1)} %convert_bitcast_fusion) | data formatting | bytes 8388608 | tf_op jit(solution)/shard_map/convert_element_type | solution.py:42
  19.4 7.9 %copy.19 = bf16[256,1,16,512]{3,2,1,0:T(8,128)(2,1)} copy(bf16[256,1,16,512]{0,3,2,1:T(8,128)(2,1)} %bitcast.31) | data formatting | bytes 8388608 | tf_op jit(solution)/shard_map/reshape | solution.py:43
  27.3 62.9 %all_to_all.15 = bf16[256,1,16,512]{3,2,1,0:T(8,128)(2,1)S(1)} all-to-all(bf16[256,1,16,512]{3,2,1,0:T(8,128)(2,1)} %copy.19), channel_id=1, replica_groups=mesh['tm'=4,'inputs'=32] {'tm','inputs'}, dimensions={0} | all-to-all | bytes 8388608 | tf_op jit(solution)/shard_map/all_to_all | solution.py:44
  90.2 0.5 copy.20
  90.7 0.4 fusion.20
  91.2 0.1 copy_negate_fusion
  91.3 0.4 maximum_bitcast_fusion
  91.7 8.6 %convolution_multiply_fusion = f32[4,2,2,512,512]{4,3,2,1,0:T(8,128)} fusion(bf16[2,4,1,512,512]{4,3,2,0,1:T(8,128)(2,1)S(1)} %maximum_bitcast_fusion, bf16[2,4,512,512,1]{3,2,1,0,4:T(8,128)(2,1)S(1)} %bitcast.29, bf16[2,4,1,512,512]{4,3,1,0,2:T(8,128)(2,1)S(1)} %bitcast.30), kind=kOutput, calls=%fused_computation | convolution fusion | flops 4315938816 | bytes 29360128 | tf_op jit(solution)/shard_map/cdpar,cdbr->dcpab/dot_general | solution.py:54
  (2 shorter events, 0.0 us)
Async XLA Ops:
  0.0 9.9 %copy-start = (f32[4,512]{1,0:T(4,128)S(1)}, f32[4,512]{1,0:T(4,128)}, u32[]{:S(2)}) copy-start(f32[4,512]{1,0:T(4,128)} %param.3) | copy-start | bytes 24580
  3.7 8.5 %collective-permute-start = (bf16[16,3,512]{2,1,0:T(4,128)(2,1)S(1)}, bf16[16,3,512]{2,1,0:T(4,128)(2,1)S(1)}, u32[]{:S(2)}, u32[]{:S(2)}) collective-permute-start(bf16[16,3,512]{2,1,0:T(4,128)(2,1)S(1)} %slice.40), channel_id=1, source_target_pairs={{0,32},{32,64},{64,96},{1,33},{33,65},{65,97},{2,34},{34,66},{66,9... | collective-permute-start | bytes 147464 | tf_op jit(solution)/shard_map/ppermute | solution.py:15
where the time goes:
time: 101 us; the launch traced here: 100 us
  blocking collectives  62.9 us (62%)
  local copies, waits for them, and re-layouts  14.8 us (15%)
  matrix products  13.5 us (13%)
  starting transfers between devices  6.21 us (6%)
  other arithmetic  2.73 us (3%)
    all_to_all x1, blocking collectives, on_device(): lax.all_to_all(spectra, ('tm', 'inputs'), split_axis=0, concat_axis=2, ti...  62.9 us
    dot_general x1, matrix products, on_device(): jnp.einsum('cdpar,cdbr->dcpab', stacked, received, preferred_element_type...  8.55 us
    reshape x1, local copies, waits for them, and re-layouts, on_device(): spectra = spectra.reshape(NFFT // 2, 1, local_inputs, 2 * spec_count)  7.91 us
    ppermute x1, starting transfers between devices, shifted(): return lax.ppermute(array, axis, pairs)  6.21 us
    dot_general x1, matrix products, on_device(): jnp.einsum('asn,nrk->kars', filtered, fourier_table(), preferred_element_...  4.94 us
    unnamed x3, local copies, waits for them, and re-layouts  3.64 us
    convert_element_type x1, local copies, waits for them, and re-layouts, on_device(): spectra = jnp.einsum('asn,nrk->kars', filtered, fourier_table(), preferre...  2.28 us
    another operation x1, other arithmetic  2.19 us
  transfers between devices with their start and end apart: 1, of which 0 were waited for; matrix products, arithmetic and copies ran while one was open for 2% of the time, Pallas kernels for 0%

commit v1 on v0

v1 whole, which is shorter than its diff:
```python
import math

import jax
import jax.numpy as jnp
import ml_dtypes
import numpy as np
from jax import lax
from jax.experimental import pallas as pl
from jax.experimental.pallas import tpu as pltpu
from jax.sharding import PartitionSpec as P

NFFT = 512
TAPS = 4
CHANNELS = NFFT // 2
LANES = 128
GROUP = 16


def fourier_rows():
    n = np.arange(NFFT)
    k = np.arange(CHANNELS)
    phase = (k[:, None] * n[None, :] % NFFT) * (2.0 * math.pi / NFFT)
    factor = 1.0 / math.sqrt(NFFT)
    rows = np.concatenate([np.cos(phase) * factor, -np.sin(phase) * factor], axis=0)
    return rows.astype(np.float32).astype(ml_dtypes.bfloat16)


def channelize_kernel(v_ref, halo_ref, taps_ref, table_ref, out_ref, past_ref, filt_ref, spec_ref):
    inputs = v_ref.shape[0]
    spectra = v_ref.shape[1] // NFFT

    @pl.when(pl.program_id(0) == 0)
    def _():
        past_ref[...] = halo_ref[...]

    for lane in range(0, NFFT, LANES):
        taps = [
            jnp.broadcast_to(taps_ref[t : t + 1, lane : lane + LANES], (inputs, LANES))
            for t in range(TAPS)
        ]
        past = tuple(
            past_ref[:, t * NFFT + lane : t * NFFT + lane + LANES].astype(jnp.float32)
            for t in range(TAPS - 1)
        )

        def step(g, past, lane=lane, taps=taps):
            window = list(past)
            rows = []
            for s in range(GROUP):
                at = pl.multiple_of((g * GROUP + s) * NFFT + lane, LANES)
                window.append(v_ref[:, pl.ds(at, LANES)].astype(jnp.float32))
                total = taps[0] * window[0]
                for t in range(1, TAPS):
                    total = total + taps[t] * window[t]
                rows.append(total.astype(jnp.bfloat16))
                window = window[1:]
            block = jnp.swapaxes(jnp.stack(rows, axis=0), 0, 1)
            first = pl.multiple_of(g * GROUP, GROUP)
            filt_ref[:, pl.ds(first, GROUP), lane : lane + LANES] = block
            return tuple(window)

        lax.fori_loop(0, spectra // GROUP, step, past)

    past_ref[...] = v_ref[:, (spectra - (TAPS - 1)) * NFFT :]

    pair = 2

    @pl.loop(0, inputs // pair)
    def _(p):
        rhs = filt_ref[pl.ds(p * pair, pair)].reshape(pair * spectra, NFFT)
        result = lax.dot_general(
            table_ref[...], rhs, (((1,), (1,)), ((), ())), preferred_element_type=jnp.float32
        ).astype(jnp.bfloat16)
        for i in range(pair):
            spec_ref[p * pair + i] = result[:, i * spectra : (i + 1) * spectra]

    @pl.loop(0, CHANNELS // GROUP)
    def _(g):
        first = pl.multiple_of(g * GROUP, GROUP)
        for r in range(2):
            block = spec_ref[:, pl.ds(r * CHANNELS + first, GROUP), :]
            out_ref[pl.ds(first, GROUP), :, r * spectra : (r + 1) * spectra] = jnp.swapaxes(
                block, 0, 1
            )


def channelize(voltages, halo, taps):
    inputs, samples = voltages.shape
    chunk = LANES
    spectra = samples // NFFT
    steps = spectra // chunk
    return pl.pallas_call(
        channelize_kernel,
        name="channelize",
        grid=(steps,),
        out_shape=jax.ShapeDtypeStruct((CHANNELS, inputs, 2 * spectra), jnp.bfloat16),
        in_specs=[
            pl.BlockSpec((inputs, chunk * NFFT), lambda c: (0, c)),
            pl.BlockSpec(halo.shape, lambda c: (0, 0)),
            pl.BlockSpec(taps.shape, lambda c: (0, 0)),
            pl.BlockSpec((NFFT, NFFT), lambda c: (0, 0)),
        ],
        out_specs=pl.BlockSpec((CHANNELS, inputs, 2 * chunk), lambda c: (0, 0, c)),
        scratch_shapes=[
            pltpu.VMEM(halo.shape, jnp.bfloat16),
            pltpu.VMEM((inputs, chunk, NFFT), jnp.bfloat16),
            pltpu.VMEM((inputs, NFFT, chunk), jnp.bfloat16),
        ],
        compiler_params=pltpu.CompilerParams(vmem_limit_bytes=40 << 20),
        cost_estimate=pl.CostEstimate(
            flops=2 * inputs * samples * NFFT, bytes_accessed=4 * inputs * samples, transcendentals=0
        ),
    )(voltages, halo, taps, jnp.asarray(fourier_rows()))


def correlate_kernel(x_ref, out_ref):
    width = x_ref.shape[-1]
    x = x_ref[...].reshape(-1, width)
    parts = []
    for at in range(0, width, 2 * LANES):
        parts.append(x[:, at + LANES : at + 2 * LANES])
        parts.append(-x[:, at : at + LANES])
    turned = jnp.concatenate(parts, axis=1)
    dims = (((1,), (1,)), ((), ()))
    scale = 2.0 / width
    real = lax.dot_general(x, x, dims, preferred_element_type=jnp.float32)
    out_ref[0, 0, 0] = real * scale
    imag = lax.dot_general(turned, x, dims, preferred_element_type=jnp.float32)
    out_ref[0, 0, 1] = imag * scale


def correlate(received):
    dumps, sources, channels, inputs, width = received.shape
    count = sources * inputs
    return pl.pallas_call(
        correlate_kernel,
        name="correlate",
        grid=(dumps, channels),
        out_shape=jax.ShapeDtypeStruct((dumps, channels, 2, count, count), jnp.float32),
        in_specs=[pl.BlockSpec((1, sources, 1, inputs, width), lambda d, c: (d, 0, c, 0, 0))],
        out_specs=pl.BlockSpec((1, 1, 2, count, count), lambda d, c: (d, c, 0, 0, 0)),
        compiler_params=pltpu.CompilerParams(vmem_limit_bytes=40 << 20),
        cost_estimate=pl.CostEstimate(
            flops=4 * dumps * channels * count * count * width,
            bytes_accessed=8 * dumps * channels * count * count,
            transcendentals=0,
        ),
    )(received)


def on_device(voltages, filter_taps):
    dumps = lax.axis_size("tm")
    sources = lax.axis_size("inputs")
    tail = voltages[:, voltages.shape[1] - (TAPS - 1) * NFFT :]
    halo = lax.ppermute(tail, "tm", [(i, i + 1) for i in range(dumps - 1)])
    spectra = channelize(voltages, halo, filter_taps)
    moved = lax.all_to_all(spectra, ("tm", "inputs"), split_axis=0, concat_axis=0, tiled=True)
    received = moved.reshape(
        dumps, sources, moved.shape[0] // (dumps * sources), moved.shape[1], moved.shape[2]
    )
    return correlate(received)


def solution(mesh):
    in_specs = (P("inputs", "tm"), P())
    out_specs = P(None, ("tm", "inputs"), None, None, None)
    return jax.shard_map(
        on_device, mesh=mesh, in_specs=in_specs, out_specs=out_specs, check_vma=False
    )
```

time: 101 us -> 96.7 us (0.957)
  Pallas kernels: 0 us -> 20.6 us
  matrix products: 13.5 us -> 0 us
  local copies, waits for them, and re-layouts: 14.8 us -> 4.73 us
  other arithmetic: 2.73 us -> 0 us
  waiting for transfers between devices: 0.01 us -> 1.16 us
    pallas_call x0 -> x2, Pallas kernels: none -> 20.6 us  [the longest x1 11.4 us: channelize(): pl.pallas_call(channelize_kernel, name='channelize', grid=(steps,), out_s...]
    dot_general x2 -> x0, matrix products: 13.5 us -> none  [the longest x1 8.55 us: on_device(): jnp.einsum('cdpar,cdbr->dcpab', stacked, received, preferred_element_type...]
    reshape x1 -> x0, local copies, waits for them, and re-layouts: 7.91 us -> none  [on_device(): spectra = spectra.reshape(NFFT // 2, 1, local_inputs, 2 * spec_count)]
    another operation x2 -> x0, other arithmetic: 2.59 us -> none
    convert_element_type x1 -> x0, local copies, waits for them, and re-layouts: 2.28 us -> none  [on_device(): spectra = jnp.einsum('asn,nrk->kars', filtered, fourier_table(), preferre...]
    ppermute x1, waiting for transfers between devices: 0.01 us -> 1.16 us  [on_device(): halo = lax.ppermute(tail, 'tm', [(i, i + 1) for i in range(dumps - 1)])]
    unnamed x3 -> x6, local copies, waits for them, and re-layouts: 3.64 us -> 3.92 us
  transfers between devices with their start and end apart: 1 -> 1, of which waited for: 0 -> 1; matrix products, arithmetic and copies ran while one was open for 2% -> 0% of each run, Pallas kernels for 0% -> 0%
where the time goes in v1:
time: 96.7 us; the launch traced here: 96.4 us
  blocking collectives  63.7 us (66%)
  Pallas kernels  20.6 us (21%)
  starting transfers between devices  6.2 us (6%)
  local copies, waits for them, and re-layouts  4.73 us (5%)
  waiting for transfers between devices  1.16 us (1%)
    all_to_all x1, blocking collectives, on_device(): lax.all_to_all(spectra, ('tm', 'inputs'), split_axis=0, concat_axis=0, ti...  63.7 us
    pallas_call x1, Pallas kernels, channelize(): pl.pallas_call(channelize_kernel, name='channelize', grid=(steps,), out_s...  11.4 us
    pallas_call x1, Pallas kernels, correlate(): pl.pallas_call(correlate_kernel, name='correlate', grid=(dumps, channels)...  9.22 us
    ppermute x1, starting transfers between devices, on_device(): halo = lax.ppermute(tail, 'tm', [(i, i + 1) for i in range(dumps - 1)])  6.2 us
    unnamed x6, local copies, waits for them, and re-layouts  3.92 us
  transfers between devices with their start and end apart: 1, of which 1 were waited for; matrix products, arithmetic and copies ran while one was open for 0% of the time, Pallas kernels for 0%

profile of v1, /device:TPU:1, one launch (start us, length us, event | category | flops | bytes accessed | tf_op | source)
XLA Modules:
  0.0 96.4 jit_solution(14902843334680329341)
XLA Ops:
  0.0 0.8 slice.3
  0.8 6.2 %collective-permute-start = (bf16[16,1536]{1,0:T(8,128)(2,1)S(1)}, bf16[16,1536]{1,0:T(8,128)(2,1)S(1)}, u32[]{:S(2)}, u32[]{:S(2)}) collective-permute-start(bf16[16,1536]{1,0:T(8,128)(2,1)S(1)} %slice.3), channel_id=1, source_target_pairs={{0,32},{32,64},{64,96},{1,33},{33,65},{65,97},{2,34},{34,66},{66,9... | collective-permute-start | bytes 147464 | tf_op jit(solution)/shard_map/ppermute | solution.py:155
  7.0 1.2 %collective-permute-done.halo_ref = bf16[16,1536]{1,0:T(8,128)(2,1)S(1)} collective-permute-done((bf16[16,1536]{1,0:T(8,128)(2,1)S(1)}, bf16[16,1536]{1,0:T(8,128)(2,1)S(1)}, u32[]{:S(2)}, u32[]{:S(2)}) %collective-permute-start) | collective-permute-done | bytes 49184 | tf_op jit(solution)/shard_map/ppermute | solution.py:155
  8.2 0.0 copy-start
  8.2 2.2 %copy-done = bf16[16,131072]{1,0:T(8,128)(2,1)S(1)} copy-done((bf16[16,131072]{1,0:T(8,128)(2,1)S(1)}, bf16[16,131072]{1,0:T(8,128)(2,1)}, u32[]{:S(2)}) %copy-start) | copy-done | bytes 4194328
  10.4 0.0 copy-start.1
  10.4 1.0 %copy-done.1 = bf16[512,512]{1,0:T(8,128)(2,1)S(1)} copy-done((bf16[512,512]{1,0:T(8,128)(2,1)S(1)}, bf16[512,512]{1,0:T(8,128)(2,1)}, u32[]{:S(2)}) %copy-start.1) | copy-done | bytes 524312
  11.4 0.0 copy-start.2
  11.4 0.7 copy-done.2
  12.1 11.4 %channelize.1 = bf16[256,16,512]{2,1,0:T(8,128)(2,1)S(1)} custom-call(bf16[16,131072]{1,0:T(8,128)(2,1)S(1)} %copy-done, bf16[16,1536]{1,0:T(8,128)(2,1)S(1)} %collective-permute-done.halo_ref, f32[4,512]{1,0:T(4,128)S(1)} %copy-done.2, bf16[512,512]{1,0:T(8,128)(2,1)S(1)} %copy-done.1), custom_call_target="tpu_custom_call" | custom-call | flops 2147483648 | bytes 8388608 | tf_op jit(solution)/shard_map/channelize/pallas_call | solution.py:92
  23.5 63.7 %all_to_all.5 = bf16[256,16,512]{2,1,0:T(8,128)(2,1)S(1)} all-to-all(bf16[256,16,512]{2,1,0:T(8,128)(2,1)S(1)} %channelize.1), channel_id=1, replica_groups=mesh['tm'=4,'inputs'=32] {'tm','inputs'}, dimensions={0} | all-to-all | bytes 8388608 | tf_op jit(solution)/shard_map/all_to_all | solution.py:157
  87.2 9.2 %correlate.1 = f32[4,2,2,512,512]{4,3,2,1,0:T(8,128)} custom-call(bf16[4,32,2,16,512]{4,3,2,1,0:T(8,128)(2,1)S(1)} %bitcast.1), custom_call_target="tpu_custom_call" | custom-call | flops 4294967296 | bytes 16777216 | tf_op jit(solution)/shard_map/correlate/pallas_call | solution.py:135
Async XLA Ops:
  0.8 7.4 %collective-permute-start = (bf16[16,1536]{1,0:T(8,128)(2,1)S(1)}, bf16[16,1536]{1,0:T(8,128)(2,1)S(1)}, u32[]{:S(2)}, u32[]{:S(2)}) collective-permute-start(bf16[16,1536]{1,0:T(8,128)(2,1)S(1)} %slice.3), channel_id=1, source_target_pairs={{0,32},{32,64},{64,96},{1,33},{33,65},{65,97},{2,34},{34,66},{66,9... | collective-permute-start | bytes 147464 | tf_op jit(solution)/shard_map/ppermute | solution.py:155
  8.2 2.2 %copy-start = (bf16[16,131072]{1,0:T(8,128)(2,1)S(1)}, bf16[16,131072]{1,0:T(8,128)(2,1)}, u32[]{:S(2)}) copy-start(bf16[16,131072]{1,0:T(8,128)(2,1)} %v_ref.1) | copy-start | bytes 12582916
  10.4 1.0 %copy-start.1 = (bf16[512,512]{1,0:T(8,128)(2,1)S(1)}, bf16[512,512]{1,0:T(8,128)(2,1)}, u32[]{:S(2)}) copy-start(bf16[512,512]{1,0:T(8,128)(2,1)} %constant.2.clone.table_ref) | copy-start | bytes 1572868
  11.4 0.7 copy-start.2

commit v2 on v0

v2 whole, which is shorter than its diff:
```python
import math

import jax
import jax.numpy as jnp
import ml_dtypes
import numpy as np
from jax import lax
from jax.experimental import pallas as pl
from jax.experimental.pallas import tpu as pltpu
from jax.sharding import PartitionSpec as P

NFFT = 512
TAPS = 4
CHANNELS = NFFT // 2
LANES = 128
GROUP = 16
PAIR = 2
UNROLL = 2
ROWS_BY_ROWS = (((1,), (1,)), ((), ()))


def fourier_rows():
    n = np.arange(NFFT)
    k = np.arange(CHANNELS)
    phase = (k[:, None] * n[None, :] % NFFT) * (2.0 * math.pi / NFFT)
    factor = 1.0 / math.sqrt(NFFT)
    rows = np.concatenate([np.cos(phase) * factor, -np.sin(phase) * factor], axis=0)
    return rows.astype(np.float32).astype(ml_dtypes.bfloat16)


def filter_group(samples_ref, first, past, taps_ref, store):
    inputs = samples_ref.shape[0]
    for lane in range(0, NFFT, LANES):
        taps = [
            jnp.broadcast_to(taps_ref[t : t + 1, lane : lane + LANES], (inputs, LANES))
            for t in range(TAPS)
        ]
        window = [past(t, lane).astype(jnp.float32) for t in range(TAPS - 1)]
        rows = []
        for s in range(GROUP):
            at = pl.multiple_of((first + s) * NFFT + lane, LANES)
            window.append(samples_ref[:, pl.ds(at, LANES)].astype(jnp.float32))
            total = taps[0] * window[0]
            for t in range(1, TAPS):
                total = total + taps[t] * window[t]
            rows.append(total.astype(jnp.bfloat16))
            window = window[1:]
        store(lane, jnp.swapaxes(jnp.stack(rows, axis=0), 0, 1))


def transform(table_ref, rows, out_ref, p):
    spectra = rows.shape[1]
    result = lax.dot_general(
        table_ref[...],
        rows.reshape(PAIR * spectra, NFFT),
        ROWS_BY_ROWS,
        preferred_element_type=jnp.float32,
    ).astype(jnp.bfloat16)
    for i in range(PAIR):
        out_ref[p * PAIR + i] = result[:, i * spectra : (i + 1) * spectra]


def swap_group(spec_ref, out_ref, g, lane):
    first = pl.multiple_of(g * GROUP, GROUP)
    for r in range(2):
        block = spec_ref[:, pl.ds(r * CHANNELS + first, GROUP), :]
        at = lane + r * LANES
        out_ref[pl.ds(first, GROUP), :, at : at + LANES] = jnp.swapaxes(block, 0, 1)


def loop(steps, body):
    @pl.loop(0, steps // UNROLL)
    def _(i):
        for u in range(UNROLL):
            body(i * UNROLL + u)


def early_kernel(
    v_hbm, taps_hbm, table_hbm, spec_ref, filt_ref, head_ref, v_ref, taps_ref, table_ref, late_ref, sems
):
    inputs = v_ref.shape[0]
    groups = v_ref.shape[1] // (GROUP * NFFT)
    half = groups // 2
    order = [(half - 1, 2)] + [(g, min(2, groups - g)) for g in range(half + 1, groups, 2)]
    order += [(g, min(2, half - 1 - g)) for g in range(0, half - 1, 2)]
    copies = [
        pltpu.make_async_copy(taps_hbm, taps_ref, sems.at[0]),
        pltpu.make_async_copy(table_hbm, table_ref, sems.at[1]),
    ]
    copies[0].start()
    parts = []
    for i, (g, count) in enumerate(order):
        span = pl.ds(g * GROUP * NFFT, count * GROUP * NFFT)
        parts.append(pltpu.make_async_copy(v_hbm.at[:, span], v_ref.at[:, span], sems.at[2 + i]))
        parts[-1].start()
        if i == 0:
            copies[1].start()
    copies[0].wait()

    def run(g, target, at):
        first = g * GROUP

        def past(t, lane):
            start = pl.multiple_of((first - (TAPS - 1) + t) * NFFT + lane, LANES)
            return v_ref[:, pl.ds(start, LANES)]

        def store(lane, block):
            target[:, pl.ds(pl.multiple_of(at * GROUP, GROUP), GROUP), lane : lane + LANES] = block

        filter_group(v_ref, first, past, taps_ref, store)

    late = groups - half
    for i, (g, count) in enumerate(order):
        if g < half - 1:
            break
        parts[i].wait()
        for q in range(count):
            if g + q >= half:
                run(g + q, late_ref, g + q - half)
    for part in parts[i:]:
        part.wait()
    copies[1].wait()
    head_ref[...] = v_ref[:, : GROUP * NFFT]

    def both(p):
        rows = late_ref[pl.ds(p * PAIR, PAIR)]
        transform(table_ref, rows, spec_ref, p)
        run(jnp.maximum(p, 1), filt_ref, jnp.maximum(p, 1))

    loop(inputs // PAIR, both)


def early(voltages, taps, table):
    inputs, samples = voltages.shape
    spectra = samples // NFFT
    any_spec = pl.BlockSpec(memory_space=pltpu.HBM)
    vmem_spec = pl.BlockSpec(memory_space=pltpu.VMEM)
    return pl.pallas_call(
        early_kernel,
        name="early",
        out_shape=(
            jax.ShapeDtypeStruct((inputs, NFFT, spectra // 2), jnp.bfloat16),
            jax.ShapeDtypeStruct((inputs, spectra // 2, NFFT), jnp.bfloat16),
            jax.ShapeDtypeStruct((inputs, GROUP * NFFT), jnp.bfloat16),
        ),
        in_specs=[any_spec] * 3,
        out_specs=(vmem_spec,) * 3,
        scratch_shapes=[
            pltpu.VMEM(voltages.shape, jnp.bfloat16),
            pltpu.VMEM(taps.shape, jnp.float32),
            pltpu.VMEM(table.shape, jnp.bfloat16),
            pltpu.VMEM((inputs, spectra // 2, NFFT), jnp.bfloat16),
            pltpu.SemaphoreType.DMA((2 + spectra // GROUP,)),
        ],
        compiler_params=pltpu.CompilerParams(vmem_limit_bytes=24 << 20),
        cost_estimate=pl.CostEstimate(
            flops=inputs * samples * NFFT, bytes_accessed=2 * inputs * samples, transcendentals=0
        ),
    )(voltages, taps, table)


def late_kernel(halo_ref, head_ref, taps_ref, table_ref, filt_ref, early_ref, out_ref, first_ref, spec_ref):
    inputs = head_ref.shape[0]

    def past(t, lane):
        return halo_ref[:, t * NFFT + lane : t * NFFT + lane + LANES]

    def store(lane, block):
        first_ref[:, :, lane : lane + LANES] = block

    filter_group(head_ref, 0, past, taps_ref, store)
    pairs = inputs // PAIR
    groups = CHANNELS // GROUP

    def both(p):
        pair = pl.ds(p * PAIR, PAIR)
        rows = jnp.concatenate([first_ref[pair], filt_ref[pair, GROUP:, :]], axis=1)
        transform(table_ref, rows, spec_ref, p)
        for q in range(groups // pairs):
            swap_group(early_ref, out_ref, p * (groups // pairs) + q, 2 * LANES)

    loop(pairs, both)

    def rest(g):
        swap_group(spec_ref, out_ref, g, 0)

    loop(groups, rest)


def late(halo, head, taps, table, filt, spec):
    inputs, spectra, _ = filt.shape
    vmem_spec = pl.BlockSpec(memory_space=pltpu.VMEM)
    return pl.pallas_call(
        late_kernel,
        name="late",
        out_shape=jax.ShapeDtypeStruct((CHANNELS, inputs, 4 * spectra), jnp.bfloat16),
        in_specs=[vmem_spec] * 6,
        out_specs=vmem_spec,
        scratch_shapes=[
            pltpu.VMEM((inputs, GROUP, NFFT), jnp.bfloat16),
            pltpu.VMEM((inputs, NFFT, spectra), jnp.bfloat16),
        ],
        compiler_params=pltpu.CompilerParams(vmem_limit_bytes=20 << 20),
        cost_estimate=pl.CostEstimate(
            flops=2 * inputs * spectra * NFFT * NFFT,
            bytes_accessed=4 * inputs * spectra * NFFT,
            transcendentals=0,
        ),
    )(halo, head, taps, table, filt, spec)


def correlate_kernel(x_ref, out_hbm, out_ref, sems):
    dumps, sources, channels, inputs, width = x_ref.shape
    scale = 2.0 / width
    copies = []

    def send(step, part):
        target = out_hbm.at[step // channels, step % channels, part]
        copies.append(pltpu.make_async_copy(out_ref.at[step, part], target, sems.at[step, part]))
        copies[-1].start()

    for step in range(dumps * channels):
        x = x_ref[step // channels, :, step % channels].reshape(sources * inputs, width)
        real = lax.dot_general(x, x, ROWS_BY_ROWS, preferred_element_type=jnp.float32)
        out_ref[step, 0] = real * scale
        send(step, 0)
        turned = []
        for at in range(0, width, 2 * LANES):
            turned += [x[:, at + LANES : at + 2 * LANES], -x[:, at : at + LANES]]
        imag = lax.dot_general(
            jnp.concatenate(turned, axis=1), x, ROWS_BY_ROWS, preferred_element_type=jnp.float32
        )
        out_ref[step, 1] = imag * scale
        send(step, 1)
    for copy in copies:
        copy.wait()


def correlate(received):
    dumps, sources, channels, inputs, width = received.shape
    count = sources * inputs
    steps = dumps * channels
    return pl.pallas_call(
        correlate_kernel,
        name="correlate",
        out_shape=jax.ShapeDtypeStruct((dumps, channels, 2, count, count), jnp.float32),
        in_specs=[pl.BlockSpec(memory_space=pltpu.VMEM)],
        out_specs=pl.BlockSpec(memory_space=pltpu.HBM),
        scratch_shapes=[
            pltpu.VMEM((steps, 2, count, count), jnp.float32),
            pltpu.SemaphoreType.DMA((steps, 2)),
        ],
        compiler_params=pltpu.CompilerParams(vmem_limit_bytes=30 << 20),
        cost_estimate=pl.CostEstimate(
            flops=4 * steps * count * count * width,
            bytes_accessed=8 * steps * count * count,
            transcendentals=0,
        ),
    )(received)


def on_device(voltages, filter_taps):
    dumps = lax.axis_size("tm")
    sources = lax.axis_size("inputs")
    table = jnp.asarray(fourier_rows())
    tail = voltages[:, voltages.shape[1] - (TAPS - 1) * NFFT :]
    halo = lax.ppermute(tail, "tm", [(i, i + 1) for i in range(dumps - 1)])
    spec, filt, head = early(
        pltpu.with_memory_space_constraint(voltages, pltpu.HBM),
        pltpu.with_memory_space_constraint(filter_taps, pltpu.HBM),
        pltpu.with_memory_space_constraint(table, pltpu.HBM),
    )
    spectra = late(halo, head, filter_taps, table, filt, spec)
    moved = lax.all_to_all(spectra, ("tm", "inputs"), split_axis=0, concat_axis=0, tiled=True)
    received = moved.reshape(
        dumps, sources, moved.shape[0] // (dumps * sources), moved.shape[1], moved.shape[2]
    )
    return correlate(received)


def solution(mesh):
    in_specs = (P("inputs", "tm"), P())
    out_specs = P(None, ("tm", "inputs"), None, None, None)
    return jax.shard_map(
        on_device, mesh=mesh, in_specs=in_specs, out_specs=out_specs, check_vma=False
    )
```

time: 101 us -> 82.5 us (0.82)
  Pallas kernels: 0 us -> 14.9 us
  local copies, waits for them, and re-layouts: 14.8 us -> 0.87 us
  matrix products: 13.5 us -> 0 us
  other arithmetic: 2.73 us -> 0 us
  blocking collectives: 62.9 us -> 60.2 us
    pallas_call x0 -> x3, Pallas kernels: none -> 14.9 us  [the longest x1 6.43 us: correlate(): pl.pallas_call(correlate_kernel, name='correlate', out_shape=jax.ShapeDty...]
    dot_general x2 -> x0, matrix products: 13.5 us -> none  [the longest x1 8.55 us: on_device(): jnp.einsum('cdpar,cdbr->dcpab', stacked, received, preferred_element_type...]
    reshape x1 -> x0, local copies, waits for them, and re-layouts: 7.91 us -> none  [on_device(): spectra = spectra.reshape(NFFT // 2, 1, local_inputs, 2 * spec_count)]
    unnamed x3 -> x4, local copies, waits for them, and re-layouts: 3.64 us -> 0.01 us
    all_to_all x1, blocking collectives: 62.9 us -> 60.2 us  [on_device(): lax.all_to_all(spectra, ('tm', 'inputs'), split_axis=0, concat_axis=0, ti...]
    another operation x2 -> x0, other arithmetic: 2.59 us -> none
    convert_element_type x1 -> x0, local copies, waits for them, and re-layouts: 2.28 us -> none  [on_device(): spectra = jnp.einsum('asn,nrk->kars', filtered, fourier_table(), preferre...]
  transfers between devices with their start and end apart: 1 -> 1, of which waited for: 0 -> 0; matrix products, arithmetic and copies ran while one was open for 2% -> 0% of each run, Pallas kernels for 0% -> 7%
where the time goes in v2:
time: 82.5 us; the launch traced here: 82.3 us
  blocking collectives  60.2 us (73%)
  Pallas kernels  14.9 us (18%)
  starting transfers between devices  6.2 us (8%)
  local copies, waits for them, and re-layouts  0.87 us (1%)
    all_to_all x1, blocking collectives, on_device(): lax.all_to_all(spectra, ('tm', 'inputs'), split_axis=0, concat_axis=0, ti...  60.2 us
    pallas_call x1, Pallas kernels, correlate(): pl.pallas_call(correlate_kernel, name='correlate', out_shape=jax.ShapeDty...  6.43 us
    ppermute x1, starting transfers between devices, on_device(): halo = lax.ppermute(tail, 'tm', [(i, i + 1) for i in range(dumps - 1)])  6.2 us
    pallas_call x1, Pallas kernels, early(): pl.pallas_call(early_kernel, name='early', out_shape=(jax.ShapeDtypeStruc...  5.37 us
    pallas_call x1, Pallas kernels, late(): pl.pallas_call(late_kernel, name='late', out_shape=jax.ShapeDtypeStruct((...  3.13 us
  transfers between devices with their start and end apart: 1, of which 0 were waited for; matrix products, arithmetic and copies ran while one was open for 0% of the time, Pallas kernels for 7%

profile of v2, /device:TPU:1, one launch (start us, length us, event | category | flops | bytes accessed | tf_op | source)
XLA Modules:
  0.0 82.3 jit_solution(12097005980046269855)
XLA Ops:
  0.0 0.0 copy-start
  0.0 0.0 copy-start.1
  0.0 0.9 %slice.3 = bf16[16,1536]{1,0:T(8,128)(2,1)S(1)} slice(bf16[16,131072]{1,0:T(8,128)(2,1)} %v_hbm.1), slice={[0:16], [129536:131072]} | slice | bytes 98304 | tf_op jit(solution)/shard_map/slice | solution.py:266
  0.9 6.2 %collective-permute-start = (bf16[16,1536]{1,0:T(8,128)(2,1)S(1)}, bf16[16,1536]{1,0:T(8,128)(2,1)S(1)}, u32[]{:S(2)}, u32[]{:S(2)}) collective-permute-start(bf16[16,1536]{1,0:T(8,128)(2,1)S(1)} %slice.3), channel_id=1, source_target_pairs={{0,32},{32,64},{64,96},{1,33},{33,65},{65,97},{2,34},{34,66},{66,9... | collective-permute-start | bytes 147464 | tf_op jit(solution)/shard_map/ppermute | solution.py:267
  7.1 5.4 %early.1 = (bf16[16,512,128]{2,1,0:T(8,128)(2,1)S(1)}, bf16[16,128,512]{2,1,0:T(8,128)(2,1)S(1)}, bf16[16,8192]{1,0:T(8,128)(2,1)S(1)}) custom-call(bf16[16,131072]{1,0:T(8,128)(2,1)} %v_hbm.1, f32[4,512]{1,0:T(4,128)} %taps_ref.1, bf16[512,512]{1,0:T(8,128)(2,1)} %constant.2.clone.table_hbm.table_ref), custom_call_target="tpu_custom_call" | custom-call | flops 1073741824 | bytes 4194304 | tf_op jit(solution)/shard_map/early/pallas_call | solution.py:138
  12.4 0.0 collective-permute-done.halo_ref
  12.5 0.0 copy-done
  12.5 0.0 copy-done.1
  12.5 3.1 %late.1 = bf16[256,16,512]{2,1,0:T(8,128)(2,1)S(1)} custom-call(bf16[16,1536]{1,0:T(8,128)(2,1)S(1)} %collective-permute-done.halo_ref, bf16[16,8192]{1,0:T(8,128)(2,1)S(1)} %get-tuple-element.8.head_ref, f32[4,512]{1,0:T(4,128)S(1)} %copy-done.1, bf16[512,512]{1,0:T(8,128)(2,1)S(1)} %copy-done, bf16[16,128,512]{2,1,0:T(8,128)(2,1)S(1)} %get-tuple-element.9.filt_ref, ...), custom_call_target="tpu_custom_call" | custom-call | flops 1073741824 | bytes 4194304 | tf_op jit(solution)/shard_map/late/pallas_call | solution.py:193
  15.6 60.2 %all_to_all.5 = bf16[256,16,512]{2,1,0:T(8,128)(2,1)S(1)} all-to-all(bf16[256,16,512]{2,1,0:T(8,128)(2,1)S(1)} %late.1), channel_id=1, replica_groups=mesh['tm'=4,'inputs'=32] {'tm','inputs'}, dimensions={0} | all-to-all | bytes 8388608 | tf_op jit(solution)/shard_map/all_to_all | solution.py:274
  75.8 6.4 %correlate.1 = f32[4,2,2,512,512]{4,3,2,1,0:T(8,128)} custom-call(bf16[4,32,2,16,512]{4,3,2,1,0:T(8,128)(2,1)S(1)} %bitcast.1), custom_call_target="tpu_custom_call" | custom-call | flops 4294967296 | bytes 16777216 | tf_op jit(solution)/shard_map/correlate/pallas_call | solution.py:243
Async XLA Ops:
  0.0 12.5 %copy-start = (bf16[512,512]{1,0:T(8,128)(2,1)S(1)}, bf16[512,512]{1,0:T(8,128)(2,1)}, u32[]{:S(2)}) copy-start(bf16[512,512]{1,0:T(8,128)(2,1)} %constant.2.clone.table_hbm.table_ref) | copy-start | bytes 1572868
  0.0 12.5 %copy-start.1 = (f32[4,512]{1,0:T(4,128)S(1)}, f32[4,512]{1,0:T(4,128)}, u32[]{:S(2)}) copy-start(f32[4,512]{1,0:T(4,128)} %taps_ref.1) | copy-start | bytes 24580
  0.9 11.6 %collective-permute-start = (bf16[16,1536]{1,0:T(8,128)(2,1)S(1)}, bf16[16,1536]{1,0:T(8,128)(2,1)S(1)}, u32[]{:S(2)}, u32[]{:S(2)}) collective-permute-start(bf16[16,1536]{1,0:T(8,128)(2,1)S(1)} %slice.3), channel_id=1, source_target_pairs={{0,32},{32,64},{64,96},{1,33},{33,65},{65,97},{2,34},{34,66},{66,9... | collective-permute-start | bytes 147464 | tf_op jit(solution)/shard_map/ppermute | solution.py:267

commit v3 on v2

--- a/solution.py
+++ b/solution.py
@@ -15,7 +15,10 @@
 LANES = 128
 GROUP = 16
 PAIR = 2
-UNROLL = 2
+FIRST_UNROLL = 2
+BOTH_UNROLL = 2
+LATE_UNROLL = 8
+REST_UNROLL = 4
 ROWS_BY_ROWS = (((1,), (1,)), ((), ()))
 
 
@@ -68,11 +71,16 @@
         out_ref[pl.ds(first, GROUP), :, at : at + LANES] = jnp.swapaxes(block, 0, 1)
 
 
-def loop(steps, body):
-    @pl.loop(0, steps // UNROLL)
+def loop(steps, body, unroll):
+    if unroll == steps:
+        for i in range(steps):
+            body(i)
+        return
+
+    @pl.loop(0, steps // unroll)
     def _(i):
-        for u in range(UNROLL):
-            body(i * UNROLL + u)
+        for u in range(unroll):
+            body(i * unroll + u)
 
 
 def early_kernel(
@@ -81,21 +89,19 @@
     inputs = v_ref.shape[0]
     groups = v_ref.shape[1] // (GROUP * NFFT)
     half = groups // 2
-    order = [(half - 1, 2)] + [(g, min(2, groups - g)) for g in range(half + 1, groups, 2)]
-    order += [(g, min(2, half - 1 - g)) for g in range(0, half - 1, 2)]
-    copies = [
-        pltpu.make_async_copy(taps_hbm, taps_ref, sems.at[0]),
-        pltpu.make_async_copy(table_hbm, table_ref, sems.at[1]),
-    ]
-    copies[0].start()
-    parts = []
-    for i, (g, count) in enumerate(order):
-        span = pl.ds(g * GROUP * NFFT, count * GROUP * NFFT)
-        parts.append(pltpu.make_async_copy(v_hbm.at[:, span], v_ref.at[:, span], sems.at[2 + i]))
-        parts[-1].start()
-        if i == 0:
-            copies[1].start()
-    copies[0].wait()
+
+    def part(g):
+        span = pl.ds(pl.multiple_of(g * GROUP * NFFT, LANES), GROUP * NFFT)
+        return pltpu.make_async_copy(v_hbm.at[:, span], v_ref.at[:, span], sems.at[g])
+
+    taps_copy = pltpu.make_async_copy(taps_hbm, taps_ref, sems.at[groups])
+    table_copy = pltpu.make_async_copy(table_hbm, table_ref, sems.at[groups + 1])
+    taps_copy.start()
+    for g in range(half - 1, groups):
+        part(g).start()
+    table_copy.start()
+    for g in range(half - 1):
+        part(g).start()
 
     def run(g, target, at):
         first = g * GROUP
@@ -109,17 +115,17 @@
 
         filter_group(v_ref, first, past, taps_ref, store)
 
-    late = groups - half
-    for i, (g, count) in enumerate(order):
-        if g < half - 1:
-            break
-        parts[i].wait()
-        for q in range(count):
-            if g + q >= half:
-                run(g + q, late_ref, g + q - half)
-    for part in parts[i:]:
-        part.wait()
-    copies[1].wait()
+    taps_copy.wait()
+    part(half - 1).wait()
+
+    def second_half(i):
+        part(half + i).wait()
+        run(half + i, late_ref, i)
+
+    loop(groups - half, second_half, FIRST_UNROLL)
+    table_copy.wait()
+    for g in range(half - 1):
+        part(g).wait()
     head_ref[...] = v_ref[:, : GROUP * NFFT]
 
     def both(p):
@@ -127,7 +133,7 @@
         transform(table_ref, rows, spec_ref, p)
         run(jnp.maximum(p, 1), filt_ref, jnp.maximum(p, 1))
 
-    loop(inputs // PAIR, both)
+    loop(inputs // PAIR, both, BOTH_UNROLL)
 
 
 def early(voltages, taps, table):
@@ -161,9 +167,11 @@
 
 def late_kernel(halo_ref, head_ref, taps_ref, table_ref, filt_ref, early_ref, out_ref, first_ref, spec_ref):
     inputs = head_ref.shape[0]
+    started = lax.axis_index("tm") > 0
 
     def past(t, lane):
-        return halo_ref[:, t * NFFT + lane : t * NFFT + lane + LANES]
+        block = halo_ref[:, t * NFFT + lane : t * NFFT + lane + LANES].astype(jnp.float32)
+        return jnp.where(started, block, 0.0)
 
     def store(lane, block):
         first_ref[:, :, lane : lane + LANES] = block
@@ -179,12 +187,12 @@
         for q in range(groups // pairs):
             swap_group(early_ref, out_ref, p * (groups // pairs) + q, 2 * LANES)
 
-    loop(pairs, both)
+    loop(pairs, both, LATE_UNROLL)
 
     def rest(g):
         swap_group(spec_ref, out_ref, g, 0)
 
-    loop(groups, rest)
+    loop(groups, rest, REST_UNROLL)
 
 
 def late(halo, head, taps, table, filt, spec):
@@ -264,7 +272,7 @@
     sources = lax.axis_size("inputs")
     table = jnp.asarray(fourier_rows())
     tail = voltages[:, voltages.shape[1] - (TAPS - 1) * NFFT :]
-    halo = lax.ppermute(tail, "tm", [(i, i + 1) for i in range(dumps - 1)])
+    halo = lax.ppermute(tail, "tm", [(i, (i + 1) % dumps) for i in range(dumps)])
     spec, filt, head = early(
         pltpu.with_memory_space_constraint(voltages, pltpu.HBM),
         pltpu.with_memory_space_constraint(filter_taps, pltpu.HBM),

time: 82.5 us -> 80.2 us (0.972)
  starting transfers between devices: 6.2 us -> 4.3 us
    ppermute x1, starting transfers between devices: 6.2 us -> 4.3 us  [on_device(): lax.ppermute(tail, 'tm', [(i, (i + 1) % dumps) for i in range(dumps)])]
where the time goes in v3:
time: 80.2 us; the launch traced here: 80 us
  blocking collectives  60.6 us (76%)
  Pallas kernels  14.2 us (18%)
  starting transfers between devices  4.3 us (5%)
  local copies, waits for them, and re-layouts  0.87 us (1%)
    all_to_all x1, blocking collectives, on_device(): lax.all_to_all(spectra, ('tm', 'inputs'), split_axis=0, concat_axis=0, ti...  60.6 us
    pallas_call x1, Pallas kernels, correlate(): pl.pallas_call(correlate_kernel, name='correlate', out_shape=jax.ShapeDty...  6.43 us
    pallas_call x1, Pallas kernels, early(): pl.pallas_call(early_kernel, name='early', out_shape=(jax.ShapeDtypeStruc...  5.33 us
    ppermute x1, starting transfers between devices, on_device(): lax.ppermute(tail, 'tm', [(i, (i + 1) % dumps) for i in range(dumps)])  4.3 us
    pallas_call x1, Pallas kernels, late(): pl.pallas_call(late_kernel, name='late', out_shape=jax.ShapeDtypeStruct((...  2.41 us
  transfers between devices with their start and end apart: 1, of which 0 were waited for; matrix products, arithmetic and copies ran while one was open for 0% of the time, Pallas kernels for 7%

profile of v3, /device:TPU:1, one launch (start us, length us, event | category | flops | bytes accessed | tf_op | source)
XLA Modules:
  0.0 80.0 jit_solution(1434980036133096100)
XLA Ops:
  0.0 0.0 copy-start
  0.0 0.0 copy-start.1
  0.0 0.9 %slice.3 = bf16[16,1536]{1,0:T(8,128)(2,1)S(1)} slice(bf16[16,131072]{1,0:T(8,128)(2,1)} %v_hbm.1), slice={[0:16], [129536:131072]} | slice | bytes 98304 | tf_op jit(solution)/shard_map/slice | solution.py:274
  0.9 4.3 %collective-permute-start = (bf16[16,1536]{1,0:T(8,128)(2,1)S(1)}, bf16[16,1536]{1,0:T(8,128)(2,1)S(1)}, u32[]{:S(2)}, u32[]{:S(2)}) collective-permute-start(bf16[16,1536]{1,0:T(8,128)(2,1)S(1)} %slice.3), channel_id=1, source_target_pairs={{0,32},{32,64},{64,96},{96,0},{1,33},{33,65},{65,97},{97,1},{2,34}... | collective-permute-start | bytes 147464 | tf_op jit(solution)/shard_map/ppermute | solution.py:275
  5.2 5.3 %early.1 = (bf16[16,512,128]{2,1,0:T(8,128)(2,1)S(1)}, bf16[16,128,512]{2,1,0:T(8,128)(2,1)S(1)}, bf16[16,8192]{1,0:T(8,128)(2,1)S(1)}) custom-call(bf16[16,131072]{1,0:T(8,128)(2,1)} %v_hbm.1, f32[4,512]{1,0:T(4,128)} %taps_ref.1, bf16[512,512]{1,0:T(8,128)(2,1)} %constant.2.clone.table_hbm.table_ref), custom_call_target="tpu_custom_call" | custom-call | flops 1073741824 | bytes 4194304 | tf_op jit(solution)/shard_map/early/pallas_call | solution.py:144
  10.5 0.0 collective-permute-done.halo_ref
  10.5 0.0 copy-done
  10.5 0.0 copy-done.1
  10.5 2.4 %late.1 = bf16[256,16,512]{2,1,0:T(8,128)(2,1)S(1)} custom-call(bf16[16,1536]{1,0:T(8,128)(2,1)S(1)} %collective-permute-done.halo_ref, bf16[16,8192]{1,0:T(8,128)(2,1)S(1)} %get-tuple-element.8.head_ref, f32[4,512]{1,0:T(4,128)S(1)} %copy-done.1, bf16[512,512]{1,0:T(8,128)(2,1)S(1)} %copy-done, bf16[16,128,512]{2,1,0:T(8,128)(2,1)S(1)} %get-tuple-element.9.filt_ref, ...), custom_call_target="tpu_custom_call" | custom-call | flops 1073741824 | bytes 4194304 | tf_op jit(solution)/shard_map/late/pallas_call | solution.py:201
  13.0 60.6 %all_to_all.5 = bf16[256,16,512]{2,1,0:T(8,128)(2,1)S(1)} all-to-all(bf16[256,16,512]{2,1,0:T(8,128)(2,1)S(1)} %late.1), channel_id=1, replica_groups=mesh['tm'=4,'inputs'=32] {'tm','inputs'}, dimensions={0} | all-to-all | bytes 8388608 | tf_op jit(solution)/shard_map/all_to_all | solution.py:282
  73.6 6.4 %correlate.1 = f32[4,2,2,512,512]{4,3,2,1,0:T(8,128)} custom-call(bf16[4,32,2,16,512]{4,3,2,1,0:T(8,128)(2,1)S(1)} %bitcast.1), custom_call_target="tpu_custom_call" | custom-call | flops 4294967296 | bytes 16777216 | tf_op jit(solution)/shard_map/correlate/pallas_call | solution.py:251
Async XLA Ops:
  0.0 10.5 %copy-start = (bf16[512,512]{1,0:T(8,128)(2,1)S(1)}, bf16[512,512]{1,0:T(8,128)(2,1)}, u32[]{:S(2)}) copy-start(bf16[512,512]{1,0:T(8,128)(2,1)} %constant.2.clone.table_hbm.table_ref) | copy-start | bytes 1572868
  0.0 10.5 %copy-start.1 = (f32[4,512]{1,0:T(4,128)S(1)}, f32[4,512]{1,0:T(4,128)}, u32[]{:S(2)}) copy-start(f32[4,512]{1,0:T(4,128)} %taps_ref.1) | copy-start | bytes 24580
  0.9 9.6 %collective-permute-start = (bf16[16,1536]{1,0:T(8,128)(2,1)S(1)}, bf16[16,1536]{1,0:T(8,128)(2,1)S(1)}, u32[]{:S(2)}, u32[]{:S(2)}) collective-permute-start(bf16[16,1536]{1,0:T(8,128)(2,1)S(1)} %slice.3), channel_id=1, source_target_pairs={{0,32},{32,64},{64,96},{96,0},{1,33},{33,65},{65,97},{97,1},{2,34}... | collective-permute-start | bytes 147464 | tf_op jit(solution)/shard_map/ppermute | solution.py:275

commit v4 on v3

--- a/solution.py
+++ b/solution.py
@@ -22,9 +22,9 @@
 ROWS_BY_ROWS = (((1,), (1,)), ((), ()))
 
 
-def fourier_rows():
+def fourier_rows(owners, groups):
     n = np.arange(NFFT)
-    k = np.arange(CHANNELS)
+    k = np.arange(CHANNELS).reshape(groups, owners, -1).transpose(1, 0, 2).reshape(-1)
     phase = (k[:, None] * n[None, :] % NFFT) * (2.0 * math.pi / NFFT)
     factor = 1.0 / math.sqrt(NFFT)
     rows = np.concatenate([np.cos(phase) * factor, -np.sin(phase) * factor], axis=0)
@@ -218,7 +218,7 @@
 
 
 def correlate_kernel(x_ref, out_hbm, out_ref, sems):
-    dumps, sources, channels, inputs, width = x_ref.shape
+    sources, dumps, channels, inputs, width = x_ref.shape
     scale = 2.0 / width
     copies = []
 
@@ -228,7 +228,7 @@
         copies[-1].start()
 
     for step in range(dumps * channels):
-        x = x_ref[step // channels, :, step % channels].reshape(sources * inputs, width)
+        x = x_ref[:, step // channels, step % channels].reshape(sources * inputs, width)
         real = lax.dot_general(x, x, ROWS_BY_ROWS, preferred_element_type=jnp.float32)
         out_ref[step, 0] = real * scale
         send(step, 0)
@@ -245,7 +245,7 @@
 
 
 def correlate(received):
-    dumps, sources, channels, inputs, width = received.shape
+    sources, dumps, channels, inputs, width = received.shape
     count = sources * inputs
     steps = dumps * channels
     return pl.pallas_call(
@@ -270,7 +270,7 @@
 def on_device(voltages, filter_taps):
     dumps = lax.axis_size("tm")
     sources = lax.axis_size("inputs")
-    table = jnp.asarray(fourier_rows())
+    table = jnp.asarray(fourier_rows(sources, dumps))
     tail = voltages[:, voltages.shape[1] - (TAPS - 1) * NFFT :]
     halo = lax.ppermute(tail, "tm", [(i, (i + 1) % dumps) for i in range(dumps)])
     spec, filt, head = early(
@@ -279,9 +279,9 @@
         pltpu.with_memory_space_constraint(table, pltpu.HBM),
     )
     spectra = late(halo, head, filter_taps, table, filt, spec)
-    moved = lax.all_to_all(spectra, ("tm", "inputs"), split_axis=0, concat_axis=0, tiled=True)
+    moved = lax.all_to_all(spectra, ("inputs", "tm"), split_axis=0, concat_axis=0, tiled=True)
     received = moved.reshape(
-        dumps, sources, moved.shape[0] // (dumps * sources), moved.shape[1], moved.shape[2]
+        sources, dumps, moved.shape[0] // (dumps * sources), moved.shape[1], moved.shape[2]
     )
     return correlate(received)
 

time: 80.2 us -> 79.4 us (0.990)
  blocking collectives: 60.6 us -> 59.7 us
    all_to_all x1, blocking collectives: 60.6 us -> 59.7 us  [on_device(): lax.all_to_all(spectra, ('inputs', 'tm'), split_axis=0, concat_axis=0, ti...]
where the time goes in v4:
time: 79.4 us; the launch traced here: 79.1 us
  blocking collectives  59.7 us (75%)
  Pallas kernels  14.2 us (18%)
  starting transfers between devices  4.3 us (5%)
  local copies, waits for them, and re-layouts  0.87 us (1%)
    all_to_all x1, blocking collectives, on_device(): lax.all_to_all(spectra, ('inputs', 'tm'), split_axis=0, concat_axis=0, ti...  59.7 us
    pallas_call x1, Pallas kernels, correlate(): pl.pallas_call(correlate_kernel, name='correlate', out_shape=jax.ShapeDty...  6.44 us
    pallas_call x1, Pallas kernels, early(): pl.pallas_call(early_kernel, name='early', out_shape=(jax.ShapeDtypeStruc...  5.33 us
    ppermute x1, starting transfers between devices, on_device(): lax.ppermute(tail, 'tm', [(i, (i + 1) % dumps) for i in range(dumps)])  4.3 us
    pallas_call x1, Pallas kernels, late(): pl.pallas_call(late_kernel, name='late', out_shape=jax.ShapeDtypeStruct((...  2.41 us
  transfers between devices with their start and end apart: 1, of which 0 were waited for; matrix products, arithmetic and copies ran while one was open for 0% of the time, Pallas kernels for 7%

profile of v4, /device:TPU:1, one launch (start us, length us, event | category | flops | bytes accessed | tf_op | source)
XLA Modules:
  0.0 79.1 jit_solution(15112951414995939400)
XLA Ops:
  0.0 0.0 copy-start
  0.0 0.0 copy-start.1
  0.0 0.9 %slice.3 = bf16[16,1536]{1,0:T(8,128)(2,1)S(1)} slice(bf16[16,131072]{1,0:T(8,128)(2,1)} %v_hbm.1), slice={[0:16], [129536:131072]} | slice | bytes 98304 | tf_op jit(solution)/shard_map/slice | solution.py:274
  0.9 4.3 %collective-permute-start = (bf16[16,1536]{1,0:T(8,128)(2,1)S(1)}, bf16[16,1536]{1,0:T(8,128)(2,1)S(1)}, u32[]{:S(2)}, u32[]{:S(2)}) collective-permute-start(bf16[16,1536]{1,0:T(8,128)(2,1)S(1)} %slice.3), channel_id=1, source_target_pairs={{0,32},{32,64},{64,96},{96,0},{1,33},{33,65},{65,97},{97,1},{2,34}... | collective-permute-start | bytes 147464 | tf_op jit(solution)/shard_map/ppermute | solution.py:275
  5.2 5.3 %early.1 = (bf16[16,512,128]{2,1,0:T(8,128)(2,1)S(1)}, bf16[16,128,512]{2,1,0:T(8,128)(2,1)S(1)}, bf16[16,8192]{1,0:T(8,128)(2,1)S(1)}) custom-call(bf16[16,131072]{1,0:T(8,128)(2,1)} %v_hbm.1, f32[4,512]{1,0:T(4,128)} %taps_ref.1, bf16[512,512]{1,0:T(8,128)(2,1)} %constant.2.clone.table_hbm.table_ref), custom_call_target="tpu_custom_call" | custom-call | flops 1073741824 | bytes 4194304 | tf_op jit(solution)/shard_map/early/pallas_call | solution.py:144
  10.5 0.0 collective-permute-done.halo_ref
  10.5 0.0 copy-done
  10.5 0.0 copy-done.1
  10.5 2.4 %late.1 = bf16[256,16,512]{2,1,0:T(8,128)(2,1)S(1)} custom-call(bf16[16,1536]{1,0:T(8,128)(2,1)S(1)} %collective-permute-done.halo_ref, bf16[16,8192]{1,0:T(8,128)(2,1)S(1)} %get-tuple-element.8.head_ref, f32[4,512]{1,0:T(4,128)S(1)} %copy-done.1, bf16[512,512]{1,0:T(8,128)(2,1)S(1)} %copy-done, bf16[16,128,512]{2,1,0:T(8,128)(2,1)S(1)} %get-tuple-element.9.filt_ref, ...), custom_call_target="tpu_custom_call" | custom-call | flops 1073741824 | bytes 4194304 | tf_op jit(solution)/shard_map/late/pallas_call | solution.py:201
  13.0 59.7 %all_to_all.5 = bf16[256,16,512]{2,1,0:T(8,128)(2,1)S(1)} all-to-all(bf16[256,16,512]{2,1,0:T(8,128)(2,1)S(1)} %late.1), channel_id=1, replica_groups=mesh['tm'=4,'inputs'=32] {'inputs','tm'}, dimensions={0} | all-to-all | bytes 8388608 | tf_op jit(solution)/shard_map/all_to_all | solution.py:282
  72.7 6.4 %correlate.1 = f32[4,2,2,512,512]{4,3,2,1,0:T(8,128)} custom-call(bf16[32,4,2,16,512]{4,3,2,1,0:T(8,128)(2,1)S(1)} %bitcast.1), custom_call_target="tpu_custom_call" | custom-call | flops 4294967296 | bytes 16777216 | tf_op jit(solution)/shard_map/correlate/pallas_call | solution.py:251
Async XLA Ops:
  0.0 10.5 %copy-start = (bf16[512,512]{1,0:T(8,128)(2,1)S(1)}, bf16[512,512]{1,0:T(8,128)(2,1)}, u32[]{:S(2)}) copy-start(bf16[512,512]{1,0:T(8,128)(2,1)} %constant.2.clone.table_hbm.table_ref) | copy-start | bytes 1572868
  0.0 10.5 %copy-start.1 = (f32[4,512]{1,0:T(4,128)S(1)}, f32[4,512]{1,0:T(4,128)}, u32[]{:S(2)}) copy-start(f32[4,512]{1,0:T(4,128)} %taps_ref.1) | copy-start | bytes 24580
  0.9 9.6 %collective-permute-start = (bf16[16,1536]{1,0:T(8,128)(2,1)S(1)}, bf16[16,1536]{1,0:T(8,128)(2,1)S(1)}, u32[]{:S(2)}, u32[]{:S(2)}) collective-permute-start(bf16[16,1536]{1,0:T(8,128)(2,1)S(1)} %slice.3), channel_id=1, source_target_pairs={{0,32},{32,64},{64,96},{96,0},{1,33},{33,65},{65,97},{97,1},{2,34}... | collective-permute-start | bytes 147464 | tf_op jit(solution)/shard_map/ppermute | solution.py:275

commit v5 on v4

--- a/solution.py
+++ b/solution.py
@@ -1,3 +1,4 @@
+import functools
 import math
 
 import jax
@@ -19,12 +20,15 @@
 BOTH_UNROLL = 2
 LATE_UNROLL = 8
 REST_UNROLL = 4
+TIME = ("yh", "core")
+INPUTS = ("z", "yl", "x")
+PEERS = ("yl", "z", "x", "core", "yh")
 ROWS_BY_ROWS = (((1,), (1,)), ((), ()))
 
 
-def fourier_rows(owners, groups):
+def fourier_rows(places):
     n = np.arange(NFFT)
-    k = np.arange(CHANNELS).reshape(groups, owners, -1).transpose(1, 0, 2).reshape(-1)
+    k = np.arange(CHANNELS).reshape(places.size, -1)[places.reshape(-1)].reshape(-1)
     phase = (k[:, None] * n[None, :] % NFFT) * (2.0 * math.pi / NFFT)
     factor = 1.0 / math.sqrt(NFFT)
     rows = np.concatenate([np.cos(phase) * factor, -np.sin(phase) * factor], axis=0)
@@ -167,7 +171,7 @@
 
 def late_kernel(halo_ref, head_ref, taps_ref, table_ref, filt_ref, early_ref, out_ref, first_ref, spec_ref):
     inputs = head_ref.shape[0]
-    started = lax.axis_index("tm") > 0
+    started = lax.axis_index(TIME) > 0
 
     def past(t, lane):
         block = halo_ref[:, t * NFFT + lane : t * NFFT + lane + LANES].astype(jnp.float32)
@@ -217,8 +221,9 @@
     )(halo, head, taps, table, filt, spec)
 
 
-def correlate_kernel(x_ref, out_hbm, out_ref, sems):
-    sources, dumps, channels, inputs, width = x_ref.shape
+def correlate_kernel(slots, x_ref, out_hbm, out_ref, sems):
+    dumps, sources = slots.shape
+    _, channels, inputs, width = x_ref.shape
     scale = 2.0 / width
     copies = []
 
@@ -228,7 +233,9 @@
         copies[-1].start()
 
     for step in range(dumps * channels):
-        x = x_ref[:, step // channels, step % channels].reshape(sources * inputs, width)
+        x = jnp.concatenate(
+            [x_ref[int(slot), step % channels] for slot in slots[step // channels]], axis=0
+        )
         real = lax.dot_general(x, x, ROWS_BY_ROWS, preferred_element_type=jnp.float32)
         out_ref[step, 0] = real * scale
         send(step, 0)
@@ -244,12 +251,13 @@
         copy.wait()
 
 
-def correlate(received):
-    sources, dumps, channels, inputs, width = received.shape
+def correlate(received, slots):
+    dumps, sources = slots.shape
+    _, channels, inputs, width = received.shape
     count = sources * inputs
     steps = dumps * channels
     return pl.pallas_call(
-        correlate_kernel,
+        functools.partial(correlate_kernel, slots),
         name="correlate",
         out_shape=jax.ShapeDtypeStruct((dumps, channels, 2, count, count), jnp.float32),
         in_specs=[pl.BlockSpec(memory_space=pltpu.VMEM)],
@@ -267,28 +275,33 @@
     )(received)
 
 
-def on_device(voltages, filter_taps):
-    dumps = lax.axis_size("tm")
-    sources = lax.axis_size("inputs")
-    table = jnp.asarray(fourier_rows(sources, dumps))
+def on_device(voltages, filter_taps, places):
+    dumps = lax.axis_size(TIME)
+    table = jnp.asarray(fourier_rows(places))
     tail = voltages[:, voltages.shape[1] - (TAPS - 1) * NFFT :]
-    halo = lax.ppermute(tail, "tm", [(i, (i + 1) % dumps) for i in range(dumps)])
+    halo = lax.ppermute(tail, TIME, [(i, (i + 1) % dumps) for i in range(dumps)])
     spec, filt, head = early(
         pltpu.with_memory_space_constraint(voltages, pltpu.HBM),
         pltpu.with_memory_space_constraint(filter_taps, pltpu.HBM),
         pltpu.with_memory_space_constraint(table, pltpu.HBM),
     )
     spectra = late(halo, head, filter_taps, table, filt, spec)
-    moved = lax.all_to_all(spectra, ("inputs", "tm"), split_axis=0, concat_axis=0, tiled=True)
-    received = moved.reshape(
-        sources, dumps, moved.shape[0] // (dumps * sources), moved.shape[1], moved.shape[2]
+    moved = lax.all_to_all(spectra, PEERS, split_axis=0, concat_axis=0, tiled=True)
+    received = moved.reshape(places.size, -1, moved.shape[1], moved.shape[2])
+    return correlate(received, np.argsort(places.reshape(-1)).reshape(dumps, -1))
+
+
+def solution(mesh):
+    sizes = dict(yh=2, core=2, z=4, yl=2, x=4)
+    names = TIME + INPUTS
+    assert mesh.devices.size == math.prod(sizes.values())
+    fine = jax.sharding.Mesh(mesh.devices.reshape([sizes[n] for n in names]), names)
+    places = np.arange(mesh.devices.size).reshape([sizes[n] for n in names])
+    places = places.transpose([names.index(n) for n in PEERS])
+    return jax.shard_map(
+        functools.partial(on_device, places=places),
+        mesh=fine,
+        in_specs=(P(INPUTS, TIME), P()),
+        out_specs=P(None, names, None, None, None),
+        check_vma=False,
     )
-    return correlate(received)
-
-
-def solution(mesh):
-    in_specs = (P("inputs", "tm"), P())
-    out_specs = P(None, ("tm", "inputs"), None, None, None)
-    return jax.shard_map(
-        on_device, mesh=mesh, in_specs=in_specs, out_specs=out_specs, check_vma=False
-    )

time: 79.4 us -> 79.4 us (level)
  no operation moved by 1% of the time
where the time goes in v5:
time: 79.4 us; the launch traced here: 79.2 us
  blocking collectives  59.8 us (75%)
  Pallas kernels  14.2 us (18%)
  starting transfers between devices  4.3 us (5%)
  local copies, waits for them, and re-layouts  0.87 us (1%)
    all_to_all x1, blocking collectives, on_device(): lax.all_to_all(spectra, PEERS, split_axis=0, concat_axis=0, tiled=True)  59.8 us
    pallas_call x1, Pallas kernels, correlate(): pl.pallas_call(functools.partial(correlate_kernel, slots), name='correlat...  6.44 us
    pallas_call x1, Pallas kernels, early(): pl.pallas_call(early_kernel, name='early', out_shape=(jax.ShapeDtypeStruc...  5.33 us
    ppermute x1, starting transfers between devices, on_device(): lax.ppermute(tail, TIME, [(i, (i + 1) % dumps) for i in range(dumps)])  4.3 us
    pallas_call x1, Pallas kernels, late(): pl.pallas_call(late_kernel, name='late', out_shape=jax.ShapeDtypeStruct((...  2.41 us
  transfers between devices with their start and end apart: 1, of which 0 were waited for; matrix products, arithmetic and copies ran while one was open for 0% of the time, Pallas kernels for 7%

profile of v5, /device:TPU:1, one launch (start us, length us, event | category | flops | bytes accessed | tf_op | source)
XLA Modules:
  0.0 79.2 jit_solution(17810326789473456113)
XLA Ops:
  0.0 0.0 copy-start
  0.0 0.0 copy-start.1
  0.0 0.9 %slice.3 = bf16[16,1536]{1,0:T(8,128)(2,1)S(1)} slice(bf16[16,131072]{1,0:T(8,128)(2,1)} %v_hbm.1), slice={[0:16], [129536:131072]} | slice | bytes 98304 | tf_op jit(solution)/shard_map/slice | solution.py:281
  0.9 4.3 %collective-permute-start = (bf16[16,1536]{1,0:T(8,128)(2,1)S(1)}, bf16[16,1536]{1,0:T(8,128)(2,1)S(1)}, u32[]{:S(2)}, u32[]{:S(2)}) collective-permute-start(bf16[16,1536]{1,0:T(8,128)(2,1)S(1)} %slice.3), channel_id=1, source_target_pairs={{0,32},{32,64},{64,96},{96,0},{1,33},{33,65},{65,97},{97,1},{2,34}... | collective-permute-start | bytes 147464 | tf_op jit(solution)/shard_map/ppermute | solution.py:282
  5.2 5.3 %early.1 = (bf16[16,512,128]{2,1,0:T(8,128)(2,1)S(1)}, bf16[16,128,512]{2,1,0:T(8,128)(2,1)S(1)}, bf16[16,8192]{1,0:T(8,128)(2,1)S(1)}) custom-call(bf16[16,131072]{1,0:T(8,128)(2,1)} %v_hbm.1, f32[4,512]{1,0:T(4,128)} %taps_ref.1, bf16[512,512]{1,0:T(8,128)(2,1)} %constant.2.clone.table_hbm.table_ref), custom_call_target="tpu_custom_call" | custom-call | flops 1073741824 | bytes 4194304 | tf_op jit(solution)/shard_map/early/pallas_call | solution.py:148
  10.5 0.0 collective-permute-done.halo_ref
  10.5 0.0 copy-done
  10.5 0.0 copy-done.1
  10.5 2.4 %late.1 = bf16[256,16,512]{2,1,0:T(8,128)(2,1)S(1)} custom-call(bf16[16,1536]{1,0:T(8,128)(2,1)S(1)} %collective-permute-done.halo_ref, bf16[16,8192]{1,0:T(8,128)(2,1)S(1)} %get-tuple-element.8.head_ref, f32[4,512]{1,0:T(4,128)S(1)} %copy-done.1, bf16[512,512]{1,0:T(8,128)(2,1)S(1)} %copy-done, bf16[16,128,512]{2,1,0:T(8,128)(2,1)S(1)} %get-tuple-element.9.filt_ref, ...), custom_call_target="tpu_custom_call" | custom-call | flops 1073741824 | bytes 4194304 | tf_op jit(solution)/shard_map/late/pallas_call | solution.py:205
  13.0 59.8 %all_to_all.5 = bf16[256,16,512]{2,1,0:T(8,128)(2,1)S(1)} all-to-all(bf16[256,16,512]{2,1,0:T(8,128)(2,1)S(1)} %late.1), channel_id=1, replica_groups=mesh['yh'=2,'core'=2,'z'=4,'yl'=2,'x'=4] {'yl','z','x','core','yh'}, dimensions={0} | all-to-all | bytes 8388608 | tf_op jit(solution)/shard_map/all_to_all | solution.py:289
  72.8 6.4 %correlate.1 = f32[4,2,2,512,512]{4,3,2,1,0:T(8,128)} custom-call(bf16[128,2,16,512]{3,2,1,0:T(8,128)(2,1)S(1)} %bitcast.1), custom_call_target="tpu_custom_call" | custom-call | flops 4294967296 | bytes 16777216 | tf_op jit(solution)/shard_map/correlate/pallas_call | solution.py:259
Async XLA Ops:
  0.0 10.5 %copy-start = (bf16[512,512]{1,0:T(8,128)(2,1)S(1)}, bf16[512,512]{1,0:T(8,128)(2,1)}, u32[]{:S(2)}) copy-start(bf16[512,512]{1,0:T(8,128)(2,1)} %constant.2.clone.table_hbm.table_ref) | copy-start | bytes 1572868
  0.0 10.5 %copy-start.1 = (f32[4,512]{1,0:T(4,128)S(1)}, f32[4,512]{1,0:T(4,128)}, u32[]{:S(2)}) copy-start(f32[4,512]{1,0:T(4,128)} %taps_ref.1) | copy-start | bytes 24580
  0.9 9.6 %collective-permute-start = (bf16[16,1536]{1,0:T(8,128)(2,1)S(1)}, bf16[16,1536]{1,0:T(8,128)(2,1)S(1)}, u32[]{:S(2)}, u32[]{:S(2)}) collective-permute-start(bf16[16,1536]{1,0:T(8,128)(2,1)S(1)} %slice.3), channel_id=1, source_target_pairs={{0,32},{32,64},{64,96},{96,0},{1,33},{33,65},{65,97},{97,1},{2,34}... | collective-permute-start | bytes 147464 | tf_op jit(solution)/shard_map/ppermute | solution.py:282

commit v6 on v5

--- a/solution.py
+++ b/solution.py
@@ -16,10 +16,10 @@
 LANES = 128
 GROUP = 16
 PAIR = 2
-FIRST_UNROLL = 2
+FIRST_UNROLL = 1
 BOTH_UNROLL = 2
 LATE_UNROLL = 8
-REST_UNROLL = 4
+REST_UNROLL = 2
 TIME = ("yh", "core")
 INPUTS = ("z", "yl", "x")
 PEERS = ("yl", "z", "x", "core", "yh")

time: 79.4 us -> 79.4 us (level)
  no operation moved by 1% of the time
where the time goes in v6:
time: 79.4 us; the launch traced here: 79.3 us
  blocking collectives  59.8 us (75%)
  Pallas kernels  14.2 us (18%)
  starting transfers between devices  4.3 us (5%)
  local copies, waits for them, and re-layouts  0.87 us (1%)
    all_to_all x1, blocking collectives, on_device(): lax.all_to_all(spectra, PEERS, split_axis=0, concat_axis=0, tiled=True)  59.8 us
    pallas_call x1, Pallas kernels, correlate(): pl.pallas_call(functools.partial(correlate_kernel, slots), name='correlat...  6.44 us
    pallas_call x1, Pallas kernels, early(): pl.pallas_call(early_kernel, name='early', out_shape=(jax.ShapeDtypeStruc...  5.32 us
    ppermute x1, starting transfers between devices, on_device(): lax.ppermute(tail, TIME, [(i, (i + 1) % dumps) for i in range(dumps)])  4.3 us
    pallas_call x1, Pallas kernels, late(): pl.pallas_call(late_kernel, name='late', out_shape=jax.ShapeDtypeStruct((...  2.45 us
  transfers between devices with their start and end apart: 1, of which 0 were waited for; matrix products, arithmetic and copies ran while one was open for 0% of the time, Pallas kernels for 7%

profile of v6, /device:TPU:1, one launch (start us, length us, event | category | flops | bytes accessed | tf_op | source)
XLA Modules:
  0.0 79.3 jit_solution(3459999890693551035)
XLA Ops:
  0.0 0.0 copy-start
  0.0 0.0 copy-start.1
  0.0 0.9 %slice.3 = bf16[16,1536]{1,0:T(8,128)(2,1)S(1)} slice(bf16[16,131072]{1,0:T(8,128)(2,1)} %v_hbm.1), slice={[0:16], [129536:131072]} | slice | bytes 98304 | tf_op jit(solution)/shard_map/slice | solution.py:281
  0.9 4.3 %collective-permute-start = (bf16[16,1536]{1,0:T(8,128)(2,1)S(1)}, bf16[16,1536]{1,0:T(8,128)(2,1)S(1)}, u32[]{:S(2)}, u32[]{:S(2)}) collective-permute-start(bf16[16,1536]{1,0:T(8,128)(2,1)S(1)} %slice.3), channel_id=1, source_target_pairs={{0,32},{32,64},{64,96},{96,0},{1,33},{33,65},{65,97},{97,1},{2,34}... | collective-permute-start | bytes 147464 | tf_op jit(solution)/shard_map/ppermute | solution.py:282
  5.2 5.3 %early.1 = (bf16[16,512,128]{2,1,0:T(8,128)(2,1)S(1)}, bf16[16,128,512]{2,1,0:T(8,128)(2,1)S(1)}, bf16[16,8192]{1,0:T(8,128)(2,1)S(1)}) custom-call(bf16[16,131072]{1,0:T(8,128)(2,1)} %v_hbm.1, f32[4,512]{1,0:T(4,128)} %taps_ref.1, bf16[512,512]{1,0:T(8,128)(2,1)} %constant.2.clone.table_hbm.table_ref), custom_call_target="tpu_custom_call" | custom-call | flops 1073741824 | bytes 4194304 | tf_op jit(solution)/shard_map/early/pallas_call | solution.py:148
  10.5 0.0 collective-permute-done.halo_ref
  10.5 0.0 copy-done
  10.5 0.0 copy-done.1
  10.5 2.5 %late.1 = bf16[256,16,512]{2,1,0:T(8,128)(2,1)S(1)} custom-call(bf16[16,1536]{1,0:T(8,128)(2,1)S(1)} %collective-permute-done.halo_ref, bf16[16,8192]{1,0:T(8,128)(2,1)S(1)} %get-tuple-element.8.head_ref, f32[4,512]{1,0:T(4,128)S(1)} %copy-done.1, bf16[512,512]{1,0:T(8,128)(2,1)S(1)} %copy-done, bf16[16,128,512]{2,1,0:T(8,128)(2,1)S(1)} %get-tuple-element.9.filt_ref, ...), custom_call_target="tpu_custom_call" | custom-call | flops 1073741824 | bytes 4194304 | tf_op jit(solution)/shard_map/late/pallas_call | solution.py:205
  13.0 59.8 %all_to_all.5 = bf16[256,16,512]{2,1,0:T(8,128)(2,1)S(1)} all-to-all(bf16[256,16,512]{2,1,0:T(8,128)(2,1)S(1)} %late.1), channel_id=1, replica_groups=mesh['yh'=2,'core'=2,'z'=4,'yl'=2,'x'=4] {'yl','z','x','core','yh'}, dimensions={0} | all-to-all | bytes 8388608 | tf_op jit(solution)/shard_map/all_to_all | solution.py:289
  72.8 6.4 %correlate.1 = f32[4,2,2,512,512]{4,3,2,1,0:T(8,128)} custom-call(bf16[128,2,16,512]{3,2,1,0:T(8,128)(2,1)S(1)} %bitcast.1), custom_call_target="tpu_custom_call" | custom-call | flops 4294967296 | bytes 16777216 | tf_op jit(solution)/shard_map/correlate/pallas_call | solution.py:259
Async XLA Ops:
  0.0 10.5 %copy-start = (bf16[512,512]{1,0:T(8,128)(2,1)S(1)}, bf16[512,512]{1,0:T(8,128)(2,1)}, u32[]{:S(2)}) copy-start(bf16[512,512]{1,0:T(8,128)(2,1)} %constant.2.clone.table_hbm.table_ref) | copy-start | bytes 1572868
  0.0 10.5 %copy-start.1 = (f32[4,512]{1,0:T(4,128)S(1)}, f32[4,512]{1,0:T(4,128)}, u32[]{:S(2)}) copy-start(f32[4,512]{1,0:T(4,128)} %taps_ref.1) | copy-start | bytes 24580
  0.9 9.6 %collective-permute-start = (bf16[16,1536]{1,0:T(8,128)(2,1)S(1)}, bf16[16,1536]{1,0:T(8,128)(2,1)S(1)}, u32[]{:S(2)}, u32[]{:S(2)}) collective-permute-start(bf16[16,1536]{1,0:T(8,128)(2,1)S(1)} %slice.3), channel_id=1, source_target_pairs={{0,32},{32,64},{64,96},{96,0},{1,33},{33,65},{65,97},{97,1},{2,34}... | collective-permute-start | bytes 147464 | tf_op jit(solution)/shard_map/ppermute | solution.py:282
